TPU v7x, 256 devices: a whole 4x4x8 slice. The times are simulated.
256 devices in a mesh: chan: 4 (over z_hi), rows: 64 (over x, z_lo, y, core).
Axes of the slice: x: 4, y: 4, z: 8 (z_hi: 4, z_lo: 2; z = z_hi * 2 + z_lo), core: 2. Of those that a mesh axis runs over, the one named last changes fastest.
Arguments:
- tokens: bfloat16 [512, 512, 512], P('rows', None, 'chan'), may hold values from -60 to 60
- gain_in: float32 [512], P('chan'), may hold values from 0.1 to 1.9
- spectral_w1: float32 [2, 8, 64, 64], P(None, 'chan'), may hold values from -0.75 to 0.75
- spectral_b1: float32 [2, 8, 64], P(None, 'chan'), may hold values from -3 to 3
- spectral_w2: float32 [2, 8, 64, 64], P(None, 'chan'), may hold values from -0.75 to 0.75
- spectral_b2: float32 [2, 8, 64], P(None, 'chan'), may hold values from -3 to 3
- gain_out: float32 [512], replicated, may hold values from 0.1 to 1.9
- fc1_weight: bfloat16 [512, 2048], P(None, 'chan'), may hold values from -0.25 to 0.25
- fc1_bias: bfloat16 [2048], P('chan'), may hold values from -3 to 3
- fc2_weight: bfloat16 [2048, 512], P('chan'), may hold values from -0.1875 to 0.1875
- fc2_bias: bfloat16 [512], P('chan'), may hold values from -3 to 3
Outputs:
- block_out: bfloat16 [512, 512, 512], P('rows', None, 'chan')
All inputs are finite; a program needn't handle non-finite values.
Results may differ from a plain program's by a relative error of at most 0.0055.
Values may be sent and summed in bfloat16 or wider, within the bound.
No kernel may reach another device: no remote copies, remote signals or barrier semaphores. Data moves between devices by JAX's collectives and lax.ppermute only.
A program may use at most 64 MiB of HBM per device.

v0:
```python
import math
import jax
import jax.numpy as jnp
from jax import lax
from jax.sharding import PartitionSpec as P

norm_eps = 1e-05
shrink_level = 0.01
highest = lax.Precision.HIGHEST


def normalize(values, gain):
    center = jnp.mean(values, axis=-1, keepdims=True)
    spread = jnp.mean(values * values, axis=-1, keepdims=True) - center * center
    return (values - center) * lax.rsqrt(spread + norm_eps) * gain


def soften(values):
    return jnp.where(
        values > shrink_level,
        values - shrink_level,
        jnp.where(values < -shrink_level, values + shrink_level, 0.0),
    )


def complex_sum(real_part, imag_part, table_cos, table_sin, form):
    first_cos = jnp.einsum(form, real_part, table_cos, precision=highest)
    first_sin = jnp.einsum(form, real_part, table_sin, precision=highest)
    second_cos = jnp.einsum(form, imag_part, table_cos, precision=highest)
    second_sin = jnp.einsum(form, imag_part, table_sin, precision=highest)
    return (first_cos - second_sin, first_sin + second_cos)


def column_transform(real_part, imag_part, sign):
    length = real_part.shape[0]
    trailing = real_part.shape[1:]
    outer_len = max((factor for factor in range(1, math.isqrt(length) + 1) if length % factor == 0))
    inner_len = length // outer_len
    real_part = real_part.reshape(outer_len, inner_len, -1)
    imag_part = imag_part.reshape(outer_len, inner_len, -1)
    outer_idx = jnp.arange(outer_len, dtype=jnp.int32)
    inner_idx = jnp.arange(inner_len, dtype=jnp.int32)
    angle = (
        2.0
        * math.pi
        / outer_len
        * (outer_idx[:, None] * outer_idx[None, :] % outer_len).astype(jnp.float32)
    )
    section_real, section_imag = complex_sum(
        real_part, imag_part, jnp.cos(angle), sign * jnp.sin(angle), "abm,ak->kbm"
    )
    twist = (
        2.0
        * math.pi
        / length
        * (outer_idx[:, None] * inner_idx[None, :] % length).astype(jnp.float32)
    )
    twist_cos = jnp.cos(twist)[:, :, None]
    twist_sin = sign * jnp.sin(twist)[:, :, None]
    section_real, section_imag = (
        section_real * twist_cos - section_imag * twist_sin,
        section_real * twist_sin + section_imag * twist_cos,
    )
    angle_two = (
        2.0
        * math.pi
        / inner_len
        * (inner_idx[:, None] * inner_idx[None, :] % inner_len).astype(jnp.float32)
    )
    final_real, final_imag = complex_sum(
        section_real, section_imag, jnp.cos(angle_two), sign * jnp.sin(angle_two), "kbm,bj->jkm"
    )
    scale = 1.0 / math.sqrt(length)
    return (
        final_real.reshape((length,) + trailing) * scale,
        final_imag.reshape((length,) + trailing) * scale,
    )


def block_matrix(weights):
    count = weights.shape[0]
    size = weights.shape[1]
    return jnp.einsum("nbo,nm->nbmo", weights, jnp.eye(count, dtype=weights.dtype)).reshape(
        count * size, count * size
    )


def spectral_layer(real_part, imag_part, weights, biases):
    weight_real = block_matrix(weights[0])
    weight_imag = block_matrix(weights[1])
    bias_real = biases[0].reshape(-1)
    bias_imag = biases[1].reshape(-1)
    real_out = (
        jnp.dot(real_part, weight_real, precision=highest)
        - jnp.dot(imag_part, weight_imag, precision=highest)
        + bias_real
    )
    imag_out = (
        jnp.dot(imag_part, weight_real, precision=highest)
        + jnp.dot(real_part, weight_imag, precision=highest)
        + bias_imag
    )
    return (real_out, imag_out)


def channel_mlp(token_rows, gain_out, first_weight, first_bias, second_weight):
    normed = normalize(token_rows.astype(jnp.float32), gain_out).astype(jnp.bfloat16)
    hidden = jax.nn.gelu(
        jnp.dot(normed, first_weight, preferred_element_type=jnp.float32)
        + first_bias.astype(jnp.float32),
        approximate=False,
    ).astype(jnp.bfloat16)
    return jnp.dot(hidden, second_weight, preferred_element_type=jnp.float32)


def local(
    tokens,
    gain_in,
    spectral_w1,
    spectral_b1,
    spectral_w2,
    spectral_b2,
    gain_out,
    fc1_weight,
    fc1_bias,
    fc2_weight,
    fc2_bias,
):
    row_count, grid_width, channels = tokens.shape
    chan_count = lax.axis_size("chan")
    all_channels = channels * chan_count
    source = tokens.astype(jnp.float32)
    totals, squares = lax.psum((jnp.sum(source, axis=2), jnp.sum(source * source, axis=2)), "chan")
    center = (totals / all_channels)[:, :, None]
    spread = (squares / all_channels)[:, :, None] - center * center
    normed = (source - center) * lax.rsqrt(spread + norm_eps) * gain_in
    half_width = grid_width // 2
    positions = jnp.arange(grid_width, dtype=jnp.int32)
    frequencies = jnp.arange(half_width, dtype=jnp.int32)
    row_scale = 1.0 / math.sqrt(grid_width)
    angle = (
        2.0
        * math.pi
        / grid_width
        * (positions[:, None] * frequencies[None, :] % grid_width).astype(jnp.float32)
    )
    forward_table = jnp.stack([jnp.cos(angle) * row_scale, -jnp.sin(angle) * row_scale])
    spectra = jnp.einsum("rwc,pwk->prkc", normed, forward_table, precision=highest)
    columns = lax.all_to_all(spectra, "rows", split_axis=2, concat_axis=1, tiled=True)
    col_real, col_imag = column_transform(columns[0], columns[1], -1.0)
    first_real, first_imag = spectral_layer(col_real, col_imag, spectral_w1, spectral_b1)
    second_real, second_imag = spectral_layer(
        jnp.maximum(first_real, 0.0), jnp.maximum(first_imag, 0.0), spectral_w2, spectral_b2
    )
    back_real, back_imag = column_transform(soften(second_real), soften(second_imag), 1.0)
    returned = lax.all_to_all(
        jnp.stack([back_real, back_imag]), "rows", split_axis=1, concat_axis=2, tiled=True
    )
    weighting = jnp.where(frequencies == 0, 1.0, 2.0).astype(jnp.float32) * row_scale
    inverse_table = jnp.stack(
        [jnp.cos(angle).T * weighting[:, None], -jnp.sin(angle).T * weighting[:, None]]
    )
    filtered = jnp.einsum("prkc,pkw->rwc", returned, inverse_table, precision=highest)
    mixed = (filtered + normed + source).astype(jnp.bfloat16)
    whole = lax.all_gather(mixed, "chan", axis=2, tiled=True)
    partial_out = channel_mlp(
        whole.reshape(-1, all_channels), gain_out, fc1_weight, fc1_bias, fc2_weight
    )
    summed = lax.psum_scatter(
        partial_out.reshape(row_count, grid_width, all_channels).astype(jnp.bfloat16),
        "chan",
        scatter_dimension=2,
        tiled=True,
    ).astype(jnp.float32)
    return (mixed.astype(jnp.float32) + summed + fc2_bias.astype(jnp.float32)).astype(jnp.bfloat16)


def solution(mesh):
    return jax.shard_map(
        local,
        mesh=mesh,
        in_specs=(
            P("rows", None, "chan"),
            P("chan"),
            P(None, "chan", None, None),
            P(None, "chan", None),
            P(None, "chan", None, None),
            P(None, "chan", None),
            P(),
            P(None, "chan"),
            P("chan"),
            P("chan", None),
            P("chan"),
        ),
        out_specs=P("rows", None, "chan"),
        check_vma=False,
    )
```

profile of v0, /device:TPU:1, one launch (start us, length us, event | category | flops | bytes accessed | tf_op | source)
XLA Modules:
  0.0 411.1 jit_solution(5114162377281175185)
XLA Ops:
  8.6 2.1 convert_reduce_fusion.1
  10.8 19.5 %all-reduce = (f32[8,512]{1,0:T(8,128)S(1)}, f32[8,512]{1,0:T(8,128)S(1)}) all-reduce(f32[8,512]{1,0:T(8,128)S(1)} %get-tuple-element.8, f32[8,512]{1,0:T(8,128)S(1)} %get-tuple-element.7), channel_id=1, replica_groups=mesh['chan'=4,'rows'=64] {'chan'}, use_global_device_ids=true, to_apply=%region_3.0 | all-reduce | flops 8192 | bytes 65536 | tf_op jit(solution)/shard_map/psum | solution.py:133
  30.3 5.5 %fusion.21 = f32[2,8,256,128]{3,2,1,0:T(8,128)S(1)} fusion(bf16[8,512,128]{2,1,0:T(8,128)(2,1)} %param.11, f32[1,512,256]{1,2,0:T(8,128)S(1)} %get-tuple-element.33, f32[1,512,256]{1,2,0:T(8,128)S(1)} %get-tuple-element.34, f32[128]{0:T(128)} %param.12, f32[8,512]{1,0:T(8,128)S(1)} %get-tuple-element.22, f32[8,512]{1,0:T(8,128)S(1)} %get-tuple-element.21), kind=kOutput, calls=%fused_computation.40 | convolution fusion | flops 3223584768 | bytes 4227584 | tf_op jit(solution)/shard_map/rwc,pwk->prkc/dot_general | solution.py:148
  35.8 2.6 copy.49
  38.3 13.0 %all-to-all-start = ((f32[2,8,256,128]{3,1,0,2:T(8,128)}), f32[2,8,256,128]{3,1,0,2:T(8,128)S(1)}, u32[]{:S(2)}, u32[]{:S(2)}) async-start(f32[2,8,256,128]{3,1,0,2:T(8,128)} %copy.49), calls=%async_computation | async-start | bytes 4194304 | tf_op jit(solution)/shard_map/all_to_all | solution.py:149
  52.7 27.2 %all-to-all-done = f32[2,8,256,128]{3,1,0,2:T(8,128)S(1)} async-done(((f32[2,8,256,128]{3,1,0,2:T(8,128)}), f32[2,8,256,128]{3,1,0,2:T(8,128)S(1)}, u32[]{:S(2)}, u32[]{:S(2)}) %all-to-all-start) | async-done | bytes 2097184 | tf_op jit(solution)/shard_map/all_to_all | solution.py:149
  88.1 2.6 fusion.63
  95.7 2.8 fusion.31
  113.4 2.5 fusion.51
  115.8 2.5 fusion.49
  124.3 3.0 multiply_add_fusion
  133.9 2.6 mul.671
  143.5 4.8 %all-to-all-start.1 = ((f32[2,512,4,128]{3,2,0,1:T(4,128)}), f32[2,512,4,128]{3,2,0,1:T(4,128)S(1)}, u32[]{:S(2)}, u32[]{:S(2)}) async-start(f32[2,512,4,128]{3,2,0,1:T(4,128)} %copy.77), calls=%async_computation.1 | async-start | bytes 4194304 | tf_op jit(solution)/shard_map/all_to_all | solution.py:156
  148.3 3.0 cosine_multiply_fusion.1
  151.3 25.9 %all-to-all-done.1 = f32[2,512,4,128]{3,2,0,1:T(4,128)S(1)} async-done(((f32[2,512,4,128]{3,2,0,1:T(4,128)}), f32[2,512,4,128]{3,2,0,1:T(4,128)S(1)}, u32[]{:S(2)}, u32[]{:S(2)}) %all-to-all-start.1) | async-done | bytes 2097184 | tf_op jit(solution)/shard_map/all_to_all | solution.py:156
  179.0 4.8 %fusion.20 = bf16[8,512,128]{2,1,0:T(8,128)(2,1)} fusion(bf16[8,512,128]{2,1,0:T(8,128)(2,1)S(1)} %copy-done.7, f32[2,8,256,128]{3,2,0,1:T(8,128)S(1)} %bitcast.137, f32[1,256,512]{1,2,0:T(8,128)S(1)} %copy-done.8, f32[1,256,512]{1,2,0:T(8,128)S(1)} %get-tuple-element.27, f32[128]{0:T(128)S(1)} %copy-done.16, f32[8,512]{1,0:T(8,128)S(1)} %get-tuple-element.22, ...), kind=kOutput, calls=%fused_computation.36 | convolution fusion | flops 3225157632 | bytes 5276160 | tf_op jit(solution)/shard_map/prkc,pkw->rwc/dot_general | solution.py:163
  184.0 84.6 %all-gather.2.cloned.1.call-done = bf16[8,512,512]{2,1,0:T(8,128)(2,1)} async-done(((bf16[8,512,128]{2,1,0:T(8,128)(2,1)}), bf16[8,512,512]{2,1,0:T(8,128)(2,1)}) %all-gather.2.cloned.1.call-update) | async-done | bytes 4194320 | tf_op jit(solution)/shard_map/all_gather | solution.py:165
  268.6 3.6 convert_reduce_fusion
  272.3 3.0 fusion.5
  275.3 24.3 %convolution_convert_fusion = bf16[4096,512]{1,0:T(8,128)(2,1)} fusion(bf16[512,512]{1,0:T(8,128)(2,1)S(1)} %copy-done, bf16[4096,512]{1,0:T(8,128)(2,1)} %fusion.5, bf16[512,512]{1,0:T(8,128)(2,1)S(1)} %copy-done.15, f32[512]{0:T(512)S(1)} %convert_element_type.156), kind=kOutput, calls=%fused_computation.24 | convolution fusion | flops 4435476480 | bytes 9439232 | tf_op jit(solution)/shard_map/dot_general | solution.py:113
  299.6 8.0 %copy.82 = bf16[8,512,512]{1,0,2:T(8,128)(2,1)} copy(bf16[8,512,512]{2,1,0:T(8,128)(2,1)} %bitcast.135) | data formatting | bytes 8388608
  307.6 6.4 %copy.86 = bf16[64,8,8,512]{3,1,2,0:T(8,128)(2,1)} copy(bf16[64,8,8,512]{3,2,1,0:T(8,128)(2,1)} %bitcast.128) | data formatting | bytes 8388608
  314.6 83.5 %reduce-scatter.4.cloned.1.call-done = bf16[128,4096]{1,0:T(8,128)(2,1)} async-done(((bf16[512,4096]{1,0:T(8,128)(2,1)}), bf16[128,4096]{1,0:T(8,128)(2,1)}) %reduce-scatter.4.cloned.1.call-update) | async-done | bytes 1048592
  398.2 2.6 copy.87
  (103 shorter events, 56.7 us)
Async XLA Ops:
  6.5 268.8 %copy-start = (bf16[512,512]{1,0:T(8,128)(2,1)S(1)}, bf16[512,512]{1,0:T(8,128)(2,1)}, u32[]{:S(2)}) copy-start(bf16[512,512]{1,0:T(8,128)(2,1)} %param.20) | copy-start | bytes 1572868
  35.7 15.6 %copy-start.9 = (f32[2,2,64,64]{3,2,1,0:T(8,128)S(1)}, f32[2,2,64,64]{3,2,1,0:T(8,128)}, u32[]{:S(2)}) copy-start(f32[2,2,64,64]{3,2,1,0:T(8,128)} %param.15) | copy-start | bytes 196612
  35.8 15.6 %copy-start.10 = (f32[2,2,64,64]{3,2,1,0:T(8,128)S(1)}, f32[2,2,64,64]{3,2,1,0:T(8,128)}, u32[]{:S(2)}) copy-start(f32[2,2,64,64]{3,2,1,0:T(8,128)} %param.13) | copy-start | bytes 196612
  35.8 16.1 %copy-start.12 = (f32[2,2,64]{2,1,0:T(2,128)S(1)}, f32[2,2,64]{2,1,0:T(2,128)}, u32[]{:S(2)}) copy-start(f32[2,2,64]{2,1,0:T(2,128)} %param.14) | copy-start | bytes 3076
  38.3 14.0 %copy-start.13 = (f32[2,2,64]{2,1,0:T(2,128)S(1)}, f32[2,2,64]{2,1,0:T(2,128)}, u32[]{:S(2)}) copy-start(f32[2,2,64]{2,1,0:T(2,128)} %param.16) | copy-start | bytes 3076
  38.3 41.5 %all-to-all-start = ((f32[2,8,256,128]{3,1,0,2:T(8,128)}), f32[2,8,256,128]{3,1,0,2:T(8,128)S(1)}, u32[]{:S(2)}, u32[]{:S(2)}) async-start(f32[2,8,256,128]{3,1,0,2:T(8,128)} %copy.49), calls=%async_computation | async-start | bytes 4194304 | tf_op jit(solution)/shard_map/all_to_all | solution.py:149
  113.3 5.0 %copy-start.5 = (f32[512,4,128]{2,0,1:T(8,128)S(1)}, f32[512,4,128]{2,0,1:T(8,128)}, u32[]{:S(2)}) copy-start(f32[512,4,128]{2,0,1:T(8,128)} %fusion.252) | copy-start | bytes 3145732
  119.5 3.3 copy-start.3
  138.1 1.9 copy-start.6
  143.5 33.8 %all-to-all-start.1 = ((f32[2,512,4,128]{3,2,0,1:T(4,128)}), f32[2,512,4,128]{3,2,0,1:T(4,128)S(1)}, u32[]{:S(2)}, u32[]{:S(2)}) async-start(f32[2,512,4,128]{3,2,0,1:T(4,128)} %copy.77), calls=%async_computation.1 | async-start | bytes 4194304 | tf_op jit(solution)/shard_map/all_to_all | solution.py:156
  148.3 120.3 %all-gather.2.cloned.1.call-start = ((), (), s32[]{:S(2)}) async-start(), calls=%async_computation.3 | async-start | bytes 5242880 | tf_op jit(solution)/shard_map/all_gather | solution.py:165
  151.3 27.7 %copy-start.16 = (f32[128]{0:T(128)S(1)}, f32[128]{0:T(128)}, u32[]{:S(2)}) copy-start(f32[128]{0:T(128)} %param.12) | copy-start | bytes 1540
  177.2 1.8 copy-start.7
  177.2 1.8 copy-start.8
  179.0 5.0 %copy-start.14 = (bf16[512]{0:T(512)(128)(2,1)S(1)}, bf16[512]{0:T(512)(128)(2,1)}, u32[]{:S(2)}) copy-start(bf16[512]{0:T(512)(128)(2,1)} %param.19) | copy-start | bytes 3076
  183.9 88.3 %copy-start.11 = (f32[512]{0:T(512)S(1)}, f32[512]{0:T(512)}, u32[]{:S(2)}) copy-start(f32[512]{0:T(512)} %param.17) | copy-start | bytes 6148
  183.9 214.2 %reduce-scatter.4.cloned.1.call-start = ((), (), s32[]{:S(2)}) async-start(), calls=%async_computation.4 | async-start | bytes 5242880
  268.6 3.7 copy-start.2
  272.2 3.1 copy-start.15
  314.0 0.7 copy-start.17
  314.0 88.7 %copy-start.4 = (bf16[8,512,128]{2,1,0:T(8,128)(2,1)S(1)}, bf16[8,512,128]{2,1,0:T(8,128)(2,1)}, u32[]{:S(2)}) copy-start(bf16[8,512,128]{2,1,0:T(8,128)(2,1)} %fusion.20) | copy-start | bytes 3145732
  314.6 89.4 %copy-start.1 = (bf16[512,512]{1,0:T(8,128)(2,1)S(1)}, bf16[512,512]{1,0:T(8,128)(2,1)}, u32[]{:S(2)}) copy-start(bf16[512,512]{1,0:T(8,128)(2,1)} %param.20) | copy-start | bytes 1572868
Sparse Core Ops, SparseCore 0:
  184.0 84.4 all-gather.1
  314.1 83.9 reduce-scatter.3
where the time goes:
time: 419 us; the launch traced here: 411 us
  waiting for transfers between devices  221 us (53%)
  matrix products  74.9 us (18%)
  local copies, waits for them, and re-layouts  46.2 us (11%)
  blocking collectives  19.5 us (5%)
  starting transfers between devices  17.9 us (4%)
  other arithmetic  17.3 us (4%)
  between operations  14.1 us (3%)
    all_gather x1, waiting for transfers between devices, local(): whole = lax.all_gather(mixed, 'chan', axis=2, tiled=True)  84.6 us
    unnamed x3, waiting for transfers between devices  83.5 us
    all_to_all x1, waiting for transfers between devices, local(): lax.all_to_all(spectra, 'rows', split_axis=2, concat_axis=1, tiled=True)  27.2 us
    all_to_all x1, waiting for transfers between devices, local(): lax.all_to_all(jnp.stack([back_real, back_imag]), 'rows', split_axis=1, c...  25.9 us
    dot_general x1, matrix products, channel_mlp(): return jnp.dot(hidden, second_weight, preferred_element_type=jnp.float32)  24.3 us
    unnamed x42, local copies, waits for them, and re-layouts  19.7 us
    psum x1, blocking collectives, local(): lax.psum((jnp.sum(source, axis=2), jnp.sum(source * source, axis=2)), 'ch...  19.5 us
    all_to_all x1, starting transfers between devices, local(): lax.all_to_all(spectra, 'rows', split_axis=2, concat_axis=1, tiled=True)  13 us
  transfers between devices with their start and end apart: 4, of which 4 were waited for; matrix products, arithmetic and copies ran while one was open for 1% of the time, Pallas kernels for 0%

commit v1 on v0

--- a/solution.py
+++ b/solution.py
@@ -162,7 +162,9 @@
     )
     filtered = jnp.einsum("prkc,pkw->rwc", returned, inverse_table, precision=highest)
     mixed = (filtered + normed + source).astype(jnp.bfloat16)
-    whole = lax.all_gather(mixed, "chan", axis=2, tiled=True)
+    whole = jnp.concatenate(
+        lax.all_to_all(jnp.stack([mixed] * lax.axis_size("chan")), "chan", 0, 0), axis=2
+    )
     partial_out = channel_mlp(
         whole.reshape(-1, all_channels), gain_out, fc1_weight, fc1_bias, fc2_weight
     )

time: 419 us -> 443 us (1.057)
  local copies, waits for them, and re-layouts: 46.2 us -> 57.2 us
  waiting for transfers between devices: 221 us -> 227 us
  starting transfers between devices: 17.9 us -> 22.4 us
    all_to_all x0 -> x1, waiting for transfers between devices: none -> 93.4 us  [local(): lax.all_to_all(jnp.stack([mixed] * lax.axis_size('chan')), 'chan', 0, 0)]
    all_gather x1 -> x0, waiting for transfers between devices: 84.6 us -> none  [local(): whole = lax.all_gather(mixed, 'chan', axis=2, tiled=True)]
    unnamed x42 -> x33, local copies, waits for them, and re-layouts: 19.7 us -> 30.6 us
    all_to_all x0 -> x1, starting transfers between devices: none -> 4.85 us  [local(): lax.all_to_all(jnp.stack([mixed] * lax.axis_size('chan')), 'chan', 0, 0)]
    unnamed x3 -> x2, waiting for transfers between devices: 83.5 us -> 80.1 us
where the time goes in v1:
time: 443 us; the launch traced here: 435 us
  waiting for transfers between devices  227 us (51%)
  matrix products  77.7 us (18%)
  local copies, waits for them, and re-layouts  57.2 us (13%)
  starting transfers between devices  22.4 us (5%)
  blocking collectives  19.5 us (4%)
  other arithmetic  17.4 us (4%)
  between operations  14.1 us (3%)
    all_to_all x1, waiting for transfers between devices, local(): lax.all_to_all(jnp.stack([mixed] * lax.axis_size('chan')), 'chan', 0, 0)  93.4 us
    unnamed x2, waiting for transfers between devices  80.1 us
    unnamed x33, local copies, waits for them, and re-layouts  30.6 us
    all_to_all x1, waiting for transfers between devices, local(): lax.all_to_all(spectra, 'rows', split_axis=2, concat_axis=1, tiled=True)  27.4 us
    all_to_all x1, waiting for transfers between devices, local(): lax.all_to_all(jnp.stack([back_real, back_imag]), 'rows', split_axis=1, c...  26 us
    dot_general x1, matrix products, channel_mlp(): return jnp.dot(hidden, second_weight, preferred_element_type=jnp.float32)  25.4 us
    psum x1, blocking collectives, local(): lax.psum((jnp.sum(source, axis=2), jnp.sum(source * source, axis=2)), 'ch...  19.5 us
    all_to_all x1, starting transfers between devices, local(): lax.all_to_all(spectra, 'rows', split_axis=2, concat_axis=1, tiled=True)  12.5 us
  transfers between devices with their start and end apart: 4, of which 4 were waited for; matrix products, arithmetic and copies ran while one was open for 1% of the time, Pallas kernels for 0%

profile of v1, /device:TPU:1, one launch (start us, length us, event | category | flops | bytes accessed | tf_op | source)
XLA Modules:
  0.0 435.2 jit_solution(381399678251147346)
XLA Ops:
  10.8 19.5 %all-reduce = (f32[8,512]{1,0:T(8,128)S(1)}, f32[8,512]{1,0:T(8,128)S(1)}) all-reduce(f32[8,512]{1,0:T(8,128)S(1)} %get-tuple-element.8, f32[8,512]{1,0:T(8,128)S(1)} %get-tuple-element.7), channel_id=1, replica_groups=mesh['chan'=4,'rows'=64] {'chan'}, use_global_device_ids=true, to_apply=%region_3.0 | all-reduce | flops 8192 | bytes 65536 | tf_op jit(solution)/shard_map/psum | solution.py:133
  30.3 5.5 %fusion.22 = f32[2,8,256,128]{3,2,1,0:T(8,128)S(1)} fusion(bf16[8,512,128]{2,1,0:T(8,128)(2,1)} %param.11, f32[1,512,256]{1,2,0:T(8,128)S(1)} %get-tuple-element.33, f32[1,512,256]{1,2,0:T(8,128)S(1)} %get-tuple-element.34, f32[128]{0:T(128)} %param.12, f32[8,512]{1,0:T(8,128)S(1)} %get-tuple-element.22, f32[8,512]{1,0:T(8,128)S(1)} %get-tuple-element.21), kind=kOutput, calls=%fused_computation.41 | convolution fusion | flops 3223584768 | bytes 4227584 | tf_op jit(solution)/shard_map/rwc,pwk->prkc/dot_general | solution.py:148
  35.8 2.6 copy.50
  38.3 12.5 %all-to-all-start = ((f32[2,8,256,128]{3,1,0,2:T(8,128)}), f32[2,8,256,128]{3,1,0,2:T(8,128)S(1)}, u32[]{:S(2)}, u32[]{:S(2)}) async-start(f32[2,8,256,128]{3,1,0,2:T(8,128)} %copy.50), calls=%async_computation | async-start | bytes 4194304 | tf_op jit(solution)/shard_map/all_to_all | solution.py:149
  52.2 27.4 %all-to-all-done = f32[2,8,256,128]{3,1,0,2:T(8,128)S(1)} async-done(((f32[2,8,256,128]{3,1,0,2:T(8,128)}), f32[2,8,256,128]{3,1,0,2:T(8,128)S(1)}, u32[]{:S(2)}, u32[]{:S(2)}) %all-to-all-start) | async-done | bytes 2097184 | tf_op jit(solution)/shard_map/all_to_all | solution.py:149
  88.0 2.6 fusion.64
  95.6 2.8 fusion.32
  121.8 2.8 convolution_subtract_fusion.1
  124.5 3.0 multiply_add_fusion
  134.1 2.5 mul.671
  142.7 4.8 %all-to-all-start.1 = ((f32[2,512,4,128]{3,2,0,1:T(4,128)}), f32[2,512,4,128]{3,2,0,1:T(4,128)S(1)}, u32[]{:S(2)}, u32[]{:S(2)}) async-start(f32[2,512,4,128]{3,2,0,1:T(4,128)} %copy.78), calls=%async_computation.1 | async-start | bytes 4194304 | tf_op jit(solution)/shard_map/all_to_all | solution.py:156
  147.5 3.0 cosine_multiply_fusion.1
  150.5 26.0 %all-to-all-done.1 = f32[2,512,4,128]{3,2,0,1:T(4,128)S(1)} async-done(((f32[2,512,4,128]{3,2,0,1:T(4,128)}), f32[2,512,4,128]{3,2,0,1:T(4,128)S(1)}, u32[]{:S(2)}, u32[]{:S(2)}) %all-to-all-start.1) | async-done | bytes 2097184 | tf_op jit(solution)/shard_map/all_to_all | solution.py:156
  178.3 4.0 fusion.21
  185.5 4.8 %all-to-all-start.2 = ((bf16[4,8,512,128]{2,1,3,0:T(8,128)(2,1)}), bf16[4,8,512,128]{2,1,3,0:T(8,128)(2,1)}, u32[]{:S(2)}, u32[]{:S(2)}) async-start(bf16[4,8,512,128]{2,1,3,0:T(8,128)(2,1)} %stack.11), calls=%async_computation.2 | async-start | bytes 8388608 | tf_op jit(solution)/shard_map/all_to_all | solution.py:166
  190.7 93.4 %all-to-all-done.2 = bf16[4,8,512,128]{2,1,3,0:T(8,128)(2,1)} async-done(((bf16[4,8,512,128]{2,1,3,0:T(8,128)(2,1)}), bf16[4,8,512,128]{2,1,3,0:T(8,128)(2,1)}, u32[]{:S(2)}, u32[]{:S(2)}) %all-to-all-start.2) | async-done | bytes 4194336 | tf_op jit(solution)/shard_map/all_to_all | solution.py:166
  284.0 3.3 bitcast_reduce_fusion
  287.4 3.4 convert_element_type.170
  290.8 11.4 %copy.86 = f32[64,8,8,512]{3,1,2,0:T(8,128)} copy(f32[64,8,8,512]{3,2,1,0:T(8,128)S(1)} %bitcast.128) | data formatting | bytes 16777216
  302.2 25.4 %convolution_convert_fusion = bf16[4096,512]{1,0:T(8,128)(2,1)} fusion(bf16[512,512]{1,0:T(8,128)(2,1)S(1)} %copy-done, bf16[512,512]{1,0:T(8,128)(2,1)S(1)} %copy-done.9, f32[4096,512]{0,1:T(8,128)} %bitcast.135, f32[512]{0:T(512)S(1)} %convert_element_type.161, f32[512]{0:T(512)S(1)} %copy-done.10, f32[4096]{0:T(1024)S(1)} %add_rsqrt_fusion, ...), kind=kOutput, calls=%fused_computation.23 | convolution fusion | flops 4443865088 | bytes 13668352 | tf_op jit(solution)/shard_map/dot_general | solution.py:113
  327.6 8.2 %copy.84 = bf16[8,512,512]{1,0,2:T(8,128)(2,1)} copy(bf16[8,512,512]{2,1,0:T(8,128)(2,1)} %bitcast.138) | data formatting | bytes 8388608
  335.8 6.5 %copy.89 = bf16[64,8,8,512]{3,1,2,0:T(8,128)(2,1)} copy(bf16[64,8,8,512]{3,2,1,0:T(8,128)(2,1)} %bitcast.130) | data formatting | bytes 8388608
  342.3 80.1 %reduce-scatter.4.cloned.1.call-done = bf16[128,4096]{1,0:T(8,128)(2,1)} async-done(((bf16[512,4096]{1,0:T(8,128)(2,1)}), bf16[128,4096]{1,0:T(8,128)(2,1)}) %reduce-scatter.4.cloned.1.call-update) | async-done | bytes 1048592
  422.4 2.6 copy.90
  (95 shorter events, 63.2 us)
Async XLA Ops:
  6.5 295.6 %copy-start = (bf16[512,512]{1,0:T(8,128)(2,1)S(1)}, bf16[512,512]{1,0:T(8,128)(2,1)}, u32[]{:S(2)}) copy-start(bf16[512,512]{1,0:T(8,128)(2,1)} %param.20) | copy-start | bytes 1572868
  6.5 44.3 %copy-start.5 = (f32[2,2,64,64]{3,2,1,0:T(8,128)S(1)}, f32[2,2,64,64]{3,2,1,0:T(8,128)}, u32[]{:S(2)}) copy-start(f32[2,2,64,64]{3,2,1,0:T(8,128)} %param.13) | copy-start | bytes 196612
  6.5 44.4 %copy-start.4 = (f32[2,2,64,64]{3,2,1,0:T(8,128)S(1)}, f32[2,2,64,64]{3,2,1,0:T(8,128)}, u32[]{:S(2)}) copy-start(f32[2,2,64,64]{3,2,1,0:T(8,128)} %param.15) | copy-start | bytes 196612
  6.5 44.9 %copy-start.6 = (f32[2,2,64]{2,1,0:T(2,128)S(1)}, f32[2,2,64]{2,1,0:T(2,128)}, u32[]{:S(2)}) copy-start(f32[2,2,64]{2,1,0:T(2,128)} %param.14) | copy-start | bytes 3076
  6.5 45.3 %copy-start.7 = (f32[2,2,64]{2,1,0:T(2,128)S(1)}, f32[2,2,64]{2,1,0:T(2,128)}, u32[]{:S(2)}) copy-start(f32[2,2,64]{2,1,0:T(2,128)} %param.16) | copy-start | bytes 3076
  38.3 41.4 %all-to-all-start = ((f32[2,8,256,128]{3,1,0,2:T(8,128)}), f32[2,8,256,128]{3,1,0,2:T(8,128)S(1)}, u32[]{:S(2)}, u32[]{:S(2)}) async-start(f32[2,8,256,128]{3,1,0,2:T(8,128)} %copy.50), calls=%async_computation | async-start | bytes 4194304 | tf_op jit(solution)/shard_map/all_to_all | solution.py:149
  141.0 37.3 %copy-start.11 = (f32[128]{0:T(128)S(1)}, f32[128]{0:T(128)}, u32[]{:S(2)}) copy-start(f32[128]{0:T(128)} %param.12) | copy-start | bytes 1540
  142.7 33.8 %all-to-all-start.1 = ((f32[2,512,4,128]{3,2,0,1:T(4,128)}), f32[2,512,4,128]{3,2,0,1:T(4,128)S(1)}, u32[]{:S(2)}, u32[]{:S(2)}) async-start(f32[2,512,4,128]{3,2,0,1:T(4,128)} %copy.78), calls=%async_computation.1 | async-start | bytes 4194304 | tf_op jit(solution)/shard_map/all_to_all | solution.py:156
  176.5 1.8 copy-start.2
  176.5 1.8 copy-start.3
  182.3 8.4 %copy-start.8 = (bf16[512]{0:T(512)(128)(2,1)S(1)}, bf16[512]{0:T(512)(128)(2,1)}, u32[]{:S(2)}) copy-start(bf16[512]{0:T(512)(128)(2,1)} %param.19) | copy-start | bytes 3076
  185.5 98.5 %all-to-all-start.2 = ((bf16[4,8,512,128]{2,1,3,0:T(8,128)(2,1)}), bf16[4,8,512,128]{2,1,3,0:T(8,128)(2,1)}, u32[]{:S(2)}, u32[]{:S(2)}) async-start(bf16[4,8,512,128]{2,1,3,0:T(8,128)(2,1)} %stack.11), calls=%async_computation.2 | async-start | bytes 8388608 | tf_op jit(solution)/shard_map/all_to_all | solution.py:166
  190.4 232.0 %reduce-scatter.4.cloned.1.call-start = ((), (), s32[]{:S(2)}) async-start(), calls=%async_computation.4 | async-start | bytes 5242880
  290.8 11.4 %copy-start.9 = (bf16[512,512]{1,0:T(8,128)(2,1)S(1)}, bf16[512,512]{1,0:T(8,128)(2,1)}, u32[]{:S(2)}) copy-start(bf16[512,512]{1,0:T(8,128)(2,1)} %param.18) | copy-start | bytes 1572868
  290.8 11.4 %copy-start.10 = (f32[512]{0:T(512)S(1)}, f32[512]{0:T(512)}, u32[]{:S(2)}) copy-start(f32[512]{0:T(512)} %param.17) | copy-start | bytes 6148
  335.7 6.5 %copy-start.12 = (bf16[128]{0:T(256)(128)(2,1)S(1)}, bf16[128]{0:T(256)(128)(2,1)}, u32[]{:S(2)}) copy-start(bf16[128]{0:T(256)(128)(2,1)} %param.21) | copy-start | bytes 772
  335.7 92.5 %copy-start.1 = (bf16[512,512]{1,0:T(8,128)(2,1)S(1)}, bf16[512,512]{1,0:T(8,128)(2,1)}, u32[]{:S(2)}) copy-start(bf16[512,512]{1,0:T(8,128)(2,1)} %param.20) | copy-start | bytes 1572868
Sparse Core Ops, SparseCore 0:
  342.4 79.9 reduce-scatter.3
